TPU v7x, 32 devices: a whole 2x2x4 slice. The times are simulated.
32 devices in a mesh: patch: 8 (over z, x), feat: 4 (over y, core).
Axes of the slice: x: 2, y: 2, z: 4, core: 2. Of those that a mesh axis runs over, the one named last changes fastest.
Arguments:
- nodes: bfloat16 [5120, 512], P(('patch', 'feat')), may hold values from -6 to 6
- edges: bfloat16 [40960, 512], P(('patch', 'feat')), may hold values from -6 to 6
- receivers: int32 [40960], P(('patch', 'feat')), may hold values from 0 to 639
- sender_slot: int32 [40960], P(('patch', 'feat')), may hold values from 0 to 831
- send_rows: int32 [8, 4, 8, 24], P('patch', 'feat'), may hold values from 0 to 159
- live_edges: int32 [32], P(('patch', 'feat')), may hold values from 1 to 1280, 30720 in all
- edge_w1: bfloat16 [1536, 512], replicated, may hold values from -0.15625 to 0.15625
- edge_b1: float32 [512], replicated, may hold values from -3 to 3
- edge_w2: bfloat16 [512, 512], replicated, may hold values from -0.25 to 0.25
- edge_gain: float32 [512], replicated, may hold values from 0.5 to 1.5
- node_w1: bfloat16 [1024, 512], replicated, may hold values from -0.1875 to 0.1875
- node_b1: float32 [512], replicated, may hold values from -3 to 3
- node_w2: bfloat16 [512, 512], replicated, may hold values from -0.25 to 0.25
- node_gain: float32 [512], replicated, may hold values from 0.5 to 1.5
Outputs:
- edges_out: bfloat16 [40960, 512], P(('patch', 'feat'))
- nodes_out: bfloat16 [5120, 512], P(('patch', 'feat'))
Inputs may be any that keep to these rules, and one draw needn't show every extreme that they name: `live_edges`: edge slots at or past a device's count are padding.
All inputs are finite; a program needn't handle non-finite values.
Results may differ from a plain program's by a relative error of at most 0.0052.
Values may be sent and summed in bfloat16 or wider, within the bound.
A program may use at most 64 MiB of HBM per device.

v0:
```python
import jax
import jax.numpy as jnp
from jax import lax
from jax.sharding import PartitionSpec as P

epsilon = 1e-05


def layer_norm(values, scales):
    average = jnp.mean(values, axis=-1, keepdims=True)
    centred = values - average
    variance = jnp.mean(centred * centred, axis=-1, keepdims=True)
    return centred * lax.rsqrt(variance + epsilon) * scales


def edge_change(edge_rows, sender_feat, receiver_feat, edge_w1, edge_b1, edge_w2, edge_gain):
    latent = edge_rows.shape[1]
    first = jnp.dot(edge_rows, edge_w1[:latent], preferred_element_type=jnp.float32)
    first = first + jnp.dot(
        sender_feat, edge_w1[latent : 2 * latent], preferred_element_type=jnp.float32
    )
    first = first + jnp.dot(
        receiver_feat, edge_w1[2 * latent :], preferred_element_type=jnp.float32
    )
    hidden = jax.nn.silu(first + edge_b1).astype(jnp.bfloat16)
    return layer_norm(jnp.dot(hidden, edge_w2, preferred_element_type=jnp.float32), edge_gain)


def node_change(node_rows, incoming, node_w1, node_b1, node_w2, node_gain):
    latent = node_rows.shape[1]
    first = jnp.dot(node_rows, node_w1[:latent], preferred_element_type=jnp.float32)
    first = first + jnp.dot(incoming, node_w1[latent:], preferred_element_type=jnp.float32)
    hidden = jax.nn.silu(first + node_b1).astype(jnp.bfloat16)
    return layer_norm(jnp.dot(hidden, node_w2, preferred_element_type=jnp.float32), node_gain)


def local(
    nodes,
    edges,
    receivers,
    sender_slot,
    send_rows,
    live_edges,
    edge_w1,
    edge_b1,
    edge_w2,
    edge_gain,
    node_w1,
    node_b1,
    node_w2,
    node_gain,
):
    latent = nodes.shape[1]
    edge_count = edges.shape[0]
    patch_rows = lax.all_gather(nodes, "feat", axis=0, tiled=True)
    patch_count = patch_rows.shape[0]
    outgoing = send_rows[0, 0]
    packed = jnp.take(nodes, outgoing.reshape(-1), axis=0).reshape(
        outgoing.shape[0], outgoing.shape[1], latent
    )
    remote = lax.all_to_all(packed, "patch", split_axis=0, concat_axis=0, tiled=True).reshape(
        -1, latent
    )
    lookup_rows = jnp.concatenate([patch_rows, remote], axis=0)
    sender_feat = jnp.take(lookup_rows, sender_slot, axis=0)
    receiver_feat = jnp.take(patch_rows, receivers, axis=0)
    alive_count = live_edges[0]
    alive = lax.broadcasted_iota(jnp.int32, (edge_count,), 0) < alive_count
    change = edge_change(edges, sender_feat, receiver_feat, edge_w1, edge_b1, edge_w2, edge_gain)
    edges_out = (edges.astype(jnp.float32) + jnp.where(alive[:, None], change, 0.0)).astype(
        jnp.bfloat16
    )
    owner_rows = lax.broadcasted_iota(jnp.int32, (patch_count, edge_count), 0)
    one_hot = ((receivers[None, :] == owner_rows) & alive[None, :]).astype(jnp.bfloat16)
    partial_sums = jnp.dot(one_hot, edges_out, preferred_element_type=jnp.float32)
    summed = lax.psum_scatter(partial_sums, "feat", scatter_dimension=0, tiled=True)
    incoming = summed.astype(jnp.bfloat16)
    change = node_change(nodes, incoming, node_w1, node_b1, node_w2, node_gain)
    nodes_out = (nodes.astype(jnp.float32) + change).astype(jnp.bfloat16)
    return (edges_out, nodes_out)


def solution(mesh):
    placed = (
        P(("patch", "feat"), None),
        P(("patch", "feat"), None),
        P(("patch", "feat")),
        P(("patch", "feat")),
        P("patch", "feat", None, None),
        P(("patch", "feat")),
        P(),
        P(),
        P(),
        P(),
        P(),
        P(),
        P(),
        P(),
    )
    return jax.shard_map(
        local,
        mesh=mesh,
        in_specs=placed,
        out_specs=(P(("patch", "feat"), None), P(("patch", "feat"), None)),
        check_vma=False,
    )
```

profile of v0, /device:TPU:0, one launch (start us, length us, event | category | flops | bytes accessed | tf_op | source)
XLA Modules:
  0.0 93.3 jit_solution(5441388097083789918)
XLA Ops:
  7.2 0.0 copy-start
  7.2 0.0 copy-start.1
  7.2 0.8 reshape_squeeze.6
  8.0 0.7 compare_and_fusion.2
  8.8 0.0 copy-start.9
  8.8 0.0 copy-start.2
  8.8 2.1 %gather_fusion = bf16[192,512]{1,0:T(8,128)(2,1)S(1)} fusion(bf16[160,512]{1,0:T(8,128)(2,1)} %param.14, s32[1024]{0:T(1024)S(1)} %pad_clamp_fusion.2), kind=kCustom, calls=%fused_computation | custom fusion | bytes 393984 | tf_op jit(solution)/shard_map/jit(_take)/gather | solution.py:58
  10.9 0.8 broadcast_select_fusion
  11.7 7.3 %all-to-all-start = ((bf16[8,24,512]{2,1,0:T(8,128)(2,1)}), bf16[8,24,512]{2,1,0:T(8,128)(2,1)S(1)}, u32[]{:S(2)}, u32[]{:S(2)}) async-start(bf16[8,24,512]{2,1,0:T(8,128)(2,1)} %broadcast_select_fusion), calls=%async_computation | async-start | bytes 393216 | tf_op jit(solution)/shard_map/all_to_all | solution.py:61
  18.9 0.0 reduce-scatter.2.cloned.1.call-start
  19.0 7.9 %all_gather.3 = bf16[640,512]{1,0:T(8,128)(2,1)S(1)} all-gather(bf16[160,512]{1,0:T(8,128)(2,1)S(1)} %copy-done.1), channel_id=1, replica_groups=mesh['patch'=8,'feat'=4] {'feat'}, dimensions={0}, use_global_device_ids=true | all-gather | bytes 819200 | tf_op jit(solution)/shard_map/all_gather | solution.py:55
  27.7 1.4 %copy.16 = bf16[1280,512]{0,1:T(8,128)(2,1)} copy(bf16[1280,512]{1,0:T(8,128)(2,1)S(1)} %copy-done.2) | data formatting | bytes 2621440 | tf_op args[1]
  29.1 4.7 %gather_fusion.2 = bf16[1280,512]{1,0:T(8,128)(2,1)} fusion(bf16[640,512]{1,0:T(8,128)(2,1)S(1)} %all_gather.3, s32[2048]{0:T(1024)S(1)} %pad_clamp_fusion), kind=kCustom, calls=%fused_computation.2 | custom fusion | bytes 2626560 | tf_op jit(solution)/shard_map/jit(_take)/gather | solution.py:66
  33.8 3.4 %fusion.25 = f32[1280,512]{1,0:T(8,128)} fusion(bf16[1280,512]{1,0:T(8,128)(2,1)S(1)} %copy-done.2, bf16[1536,512]{1,0:T(8,128)(2,1)} %param.20), kind=kOutput, calls=%fused_computation.31 | convolution fusion | flops 671088640 | bytes 4456448 | tf_op jit(solution)/shard_map/dot_general | solution.py:18
  37.2 0.7 copy-done.6
  37.9 1.0 %pad_maximum_fusion = bf16[832,512]{1,0:T(8,128)(2,1)S(1)} fusion(bf16[192,512]{1,0:T(8,128)(2,1)} %bitcast.17, bf16[640,512]{1,0:T(8,128)(2,1)S(1)} %all_gather.3), kind=kLoop, calls=%fused_computation.23 | loop fusion | flops 1703936 | bytes 1703936 | tf_op jit(solution)/shard_map/concatenate | solution.py:64
  38.9 4.1 %gather_fusion.1 = bf16[1280,512]{1,0:T(8,128)(2,1)S(1)} fusion(bf16[832,512]{1,0:T(8,128)(2,1)S(1)} %pad_maximum_fusion, s32[2048]{0:T(1024)S(1)} %pad_clamp_fusion.1), kind=kCustom, calls=%fused_computation.1 | custom fusion | bytes 2626560 | tf_op jit(solution)/shard_map/jit(_take)/gather | solution.py:65
  43.0 4.3 %convolution_add_fusion.1 = f32[1280,512]{1,0:T(8,128)} fusion(f32[1280,512]{1,0:T(8,128)} %fusion.25, bf16[1280,512]{1,0:T(8,128)(2,1)S(1)} %gather_fusion.1, pred[1280]{0:T(1024)(128)(4,1)S(1)} %compare_and_fusion.1, bf16[1536,512]{1,0:T(8,128)(2,1)} %param.20), kind=kOutput, calls=%fused_computation.5 | convolution fusion | flops 672399360 | bytes 7079168 | tf_op jit(solution)/shard_map/dot_general | solution.py:19
  47.4 4.1 %fusion.41 = (f32[1280]{0:T(1024)S(1)}, f32[1280,512]{0,1:T(8,128)S(1)}) fusion(bf16[512,512]{1,0:T(8,128)(2,1)S(1)} %copy-done, f32[1280,512]{1,0:T(8,128)} %convolution_add_fusion.1, f32[512]{0:T(512)S(1)} %copy-done.12, bf16[1280,512]{1,0:T(8,128)(2,1)} %gather_fusion.2, pred[1280]{0:T(1024)(128)(4,1)S(1)} %compare_and_fusion, bf16[1536,512]{1,0:T(8,128)(2,1)} %param.20), kind=kOutput, calls=%fused_computation.60 | convolution fusion | flops 1348074240 | bytes 7610624 | tf_op jit(solution)/shard_map/dot_general | solution.py:26
  51.5 0.3 multiply_reduce_fusion
  51.8 1.0 %copy-done.3 = bf16[1280,512]{0,1:T(8,128)(2,1)S(1)} copy-done((bf16[1280,512]{0,1:T(8,128)(2,1)S(1)}, bf16[1280,512]{0,1:T(8,128)(2,1)}, u32[]{:S(2)}) %copy-start.3) | copy-done | bytes 1310744
  52.8 0.6 add_convert_fusion
  53.4 1.0 %copy-done.4 = bf16[1280,512]{0,1:T(8,128)(2,1)} copy-done((bf16[1280,512]{0,1:T(8,128)(2,1)}, bf16[1280,512]{0,1:T(8,128)(2,1)S(1)}, u32[]{:S(2)}) %copy-start.4) | copy-done | bytes 1310744
  54.5 2.1 %fusion.2 = f32[640,512]{1,0:T(8,128)} fusion(bf16[1280,512]{0,1:T(8,128)(2,1)S(1)} %add_convert_fusion, s32[1280]{0:T(1024)S(1)} %copy-done.9, pred[1280]{0:T(1024)(128)(4,1)S(1)} %iota_compare_fusion.1), kind=kOutput, calls=%fused_computation.8 | convolution fusion | flops 840499200 | bytes 2627840 | tf_op jit(solution)/shard_map/dot_general | solution.py:75
  56.6 0.0 reduce-scatter.2.cloned.1.call-update
  56.7 0.2 fusion.20
  56.9 1.0 %copy-done.5 = bf16[1280,512]{0,1:T(8,128)(2,1)S(1)} copy-done((bf16[1280,512]{0,1:T(8,128)(2,1)S(1)}, bf16[1280,512]{0,1:T(8,128)(2,1)}, u32[]{:S(2)}) %copy-start.5) | copy-done | bytes 1310744
  57.9 1.5 %copy.17 = bf16[1280,512]{1,0:T(8,128)(2,1)} copy(bf16[1280,512]{0,1:T(8,128)(2,1)S(1)} %copy-done.5) | data formatting | bytes 2621440
  59.4 24.3 %reduce-scatter.2.cloned.1.call-done = f32[160,512]{1,0:T(8,128)} async-done(((f32[640,512]{1,0:T(8,128)}), f32[160,512]{1,0:T(8,128)}) %reduce-scatter.2.cloned.1.call-update) | async-done | bytes 327696 | tf_op jit(solution)/shard_map/reduce_scatter | solution.py:76
  83.7 1.7 %fusion.46 = (f32[160]{0:T(256)S(1)}, f32[160,512]{1,0:T(8,128)S(1)}) fusion(bf16[512,512]{1,0:T(8,128)(2,1)} %param.26, f32[160,512]{1,0:T(8,128)S(1)} %fusion.20, bf16[1024,512]{1,0:T(8,128)(2,1)S(1)} %copy-done.7, f32[512]{0:T(512)S(1)} %copy-done.13, f32[160,512]{1,0:T(8,128)} %reduce-scatter.2.cloned.1.call-done), kind=kOutput, calls=%fused_computation.61 | convolution fusion | flops 168509280 | bytes 2034304 | tf_op jit(solution)/shard_map/dot_general | solution.py:34
  85.5 0.2 multiply_reduce_fusion.1
  85.7 0.8 add_convert_fusion.1
  (34 shorter events, 0.1 us)
Async XLA Ops:
  7.2 40.2 %copy-start = (bf16[512,512]{1,0:T(8,128)(2,1)S(1)}, bf16[512,512]{1,0:T(8,128)(2,1)}, u32[]{:S(2)}) copy-start(bf16[512,512]{1,0:T(8,128)(2,1)} %param.22) | copy-start | bytes 1572868
  7.2 11.8 %copy-start.1 = (bf16[160,512]{1,0:T(8,128)(2,1)S(1)}, bf16[160,512]{1,0:T(8,128)(2,1)}, u32[]{:S(2)}) copy-start(bf16[160,512]{1,0:T(8,128)(2,1)} %param.14) | copy-start | bytes 491524
  8.7 18.2 %copy-start.8 = (s32[1280]{0:T(1024)S(1)}, s32[1280]{0:T(1024)}, u32[]{:S(2)}) copy-start(s32[1280]{0:T(1024)} %param.17) | copy-start | bytes 15364
  8.8 18.2 %copy-start.9 = (s32[1280]{0:T(1024)S(1)}, s32[1280]{0:T(1024)}, u32[]{:S(2)}) copy-start(s32[1280]{0:T(1024)} %param.16) | copy-start | bytes 15364
  8.8 18.9 %copy-start.2 = (bf16[1280,512]{1,0:T(8,128)(2,1)S(1)}, bf16[1280,512]{1,0:T(8,128)(2,1)}, u32[]{:S(2)}) copy-start(bf16[1280,512]{1,0:T(8,128)(2,1)} %param.15) | copy-start | bytes 3932164
  11.7 25.6 %all-to-all-start = ((bf16[8,24,512]{2,1,0:T(8,128)(2,1)}), bf16[8,24,512]{2,1,0:T(8,128)(2,1)S(1)}, u32[]{:S(2)}, u32[]{:S(2)}) async-start(bf16[8,24,512]{2,1,0:T(8,128)(2,1)} %broadcast_select_fusion), calls=%async_computation | async-start | bytes 393216 | tf_op jit(solution)/shard_map/all_to_all | solution.py:61
  18.9 64.8 %reduce-scatter.2.cloned.1.call-start = ((), (), s32[]{:S(2)}) async-start(), calls=%async_computation.2 | async-start | bytes 1638400 | tf_op jit(solution)/shard_map/reduce_scatter | solution.py:76
  37.2 0.7 copy-start.6
  43.0 4.4 %copy-start.12 = (f32[512]{0:T(512)S(1)}, f32[512]{0:T(512)}, u32[]{:S(2)}) copy-start(f32[512]{0:T(512)} %param.21) | copy-start | bytes 6148
  51.5 1.3 %copy-start.3 = (bf16[1280,512]{0,1:T(8,128)(2,1)S(1)}, bf16[1280,512]{0,1:T(8,128)(2,1)}, u32[]{:S(2)}) copy-start(bf16[1280,512]{0,1:T(8,128)(2,1)} %copy.16) | copy-start | bytes 3932164
  51.5 1.3 %copy-start.10 = (f32[512]{0:T(512)S(1)}, f32[512]{0:T(512)}, u32[]{:S(2)}) copy-start(f32[512]{0:T(512)} %param.23) | copy-start | bytes 6148
  53.4 1.1 %copy-start.4 = (bf16[1280,512]{0,1:T(8,128)(2,1)}, bf16[1280,512]{0,1:T(8,128)(2,1)S(1)}, u32[]{:S(2)}) copy-start(bf16[1280,512]{0,1:T(8,128)(2,1)S(1)} %add_convert_fusion) | copy-start | bytes 3932164
  54.5 2.2 %copy-start.7 = (bf16[1024,512]{1,0:T(8,128)(2,1)S(1)}, bf16[1024,512]{1,0:T(8,128)(2,1)}, u32[]{:S(2)}) copy-start(bf16[1024,512]{1,0:T(8,128)(2,1)} %param.24) | copy-start | bytes 3145732
  56.6 1.3 %copy-start.5 = (bf16[1280,512]{0,1:T(8,128)(2,1)S(1)}, bf16[1280,512]{0,1:T(8,128)(2,1)}, u32[]{:S(2)}) copy-start(bf16[1280,512]{0,1:T(8,128)(2,1)} %copy-done.4) | copy-start | bytes 3932164
  56.7 27.0 %copy-start.13 = (f32[512]{0:T(512)S(1)}, f32[512]{0:T(512)}, u32[]{:S(2)}) copy-start(f32[512]{0:T(512)} %param.25) | copy-start | bytes 6148
  59.4 26.3 %copy-start.11 = (f32[512]{0:T(512)S(1)}, f32[512]{0:T(512)}, u32[]{:S(2)}) copy-start(f32[512]{0:T(512)} %param.27) | copy-start | bytes 6148
Sparse Core Ops, SparseCore 0:
  56.8 26.8 reduce-scatter.1
where the time goes:
time: 93.8 us; the launch traced here: 93.3 us
  waiting for transfers between devices  24.3 us (26%)
  local copies, waits for them, and re-layouts  18.5 us (20%)
  matrix products  16 us (17%)
  between operations  14.9 us (16%)
  blocking collectives  7.91 us (8%)
  starting transfers between devices  7.32 us (8%)
  other arithmetic  4.5 us (5%)
    reduce_scatter x1, waiting for transfers between devices, local(): lax.psum_scatter(partial_sums, 'feat', scatter_dimension=0, tiled=True)  24.3 us
    all_gather x1, blocking collectives, local(): patch_rows = lax.all_gather(nodes, 'feat', axis=0, tiled=True)  7.91 us
    all_to_all x1, starting transfers between devices, local(): lax.all_to_all(packed, 'patch', split_axis=0, concat_axis=0, tiled=True)  7.28 us
    unnamed x30, local copies, waits for them, and re-layouts  6.7 us
    gather x1, local copies, waits for them, and re-layouts, local(): receiver_feat = jnp.take(patch_rows, receivers, axis=0)  4.72 us
    dot_general x1, matrix products, edge_change(): jnp.dot(sender_feat, edge_w1[latent:2 * latent], preferred_element_type=j...  4.35 us
    gather x1, local copies, waits for them, and re-layouts, local(): sender_feat = jnp.take(lookup_rows, sender_slot, axis=0)  4.1 us
    dot_general x1, matrix products, edge_change(): jnp.dot(hidden, edge_w2, preferred_element_type=jnp.float32)  4.08 us
  transfers between devices with their start and end apart: 2, of which 1 were waited for; matrix products, arithmetic and copies ran while one was open for 12% of the time, Pallas kernels for 0%

commit v1 on v0

v1 whole, which is shorter than its diff:
```python
import functools

import jax
import jax.numpy as jnp
from jax import lax
from jax.experimental import pallas as pl
from jax.experimental.pallas import tpu as pltpu
from jax.sharding import PartitionSpec as P

epsilon = 1e-05
MESH = pl.DeviceIdType.MESH
LANES = 128
F32, BF16 = jnp.float32, jnp.bfloat16


def dot(a, b):
    return jnp.dot(a, b, preferred_element_type=F32)


def layer_norm(values, scales):
    average = jnp.mean(values, axis=-1, keepdims=True)
    centred = values - average
    variance = jnp.mean(centred * centred, axis=-1, keepdims=True)
    return centred * lax.rsqrt(variance + epsilon) * scales


def column(row):
    parts = []
    for at in range(0, row.shape[1], LANES):
        block = jnp.broadcast_to(row[:, at : at + LANES], (LANES, LANES))
        parts.append(block.T[:, :1])
    return jnp.concatenate(parts, axis=0)


def mask(hit):
    return jnp.where(hit, 1.0, 0.0).astype(BF16)


def low_bit(number):
    return number & -number


def kernel(
    n_patch,
    n_feat,
    cap,
    tile,
    live_ref,
    nodes_ref,
    recv_ref,
    slot_ref,
    list_ref,
    b1_ref,
    gain_ref,
    nb1_ref,
    ngain_ref,
    edges_hbm,
    w1_hbm,
    w2_hbm,
    nw1_hbm,
    nw2_hbm,
    edges_out,
    nodes_out,
    edges_v,
    w1,
    w2,
    nw1,
    nw2,
    packed,
    remote,
    patch,
    table,
    first,
    out_v,
    send_v,
    got_v,
    load_sem,
    store_sem,
    list_send,
    list_recv,
    node_send,
    node_recv,
    sum_send,
    sum_recv,
):
    me_p, me_f = lax.axis_index("patch"), lax.axis_index("feat")
    own, latent = nodes_ref.shape
    count = edges_v.shape[0]
    slots = packed.shape[1]
    n_local = n_feat * own
    n_table = n_local + n_patch * slots
    bits = [1 << i for i in range(n_feat.bit_length() - 1)]

    def feat_peer(bit):
        return jnp.bitwise_xor(me_f, bit)

    def patch_peer(step):
        return lax.rem(me_p + step, n_patch)

    barrier = pltpu.get_barrier_semaphore()
    for bit in bits:
        pl.semaphore_signal(
            barrier, inc=1, device_id=(me_p, feat_peer(bit)), device_id_type=MESH
        )
    for step in range(1, n_patch):
        pl.semaphore_signal(
            barrier, inc=1, device_id=(patch_peer(step), me_f), device_id_type=MESH
        )

    loads = []
    for i, (src, dst) in enumerate(
        ((w1_hbm, w1), (edges_hbm, edges_v), (w2_hbm, w2), (nw1_hbm, nw1), (nw2_hbm, nw2))
    ):
        loads.append(pltpu.make_async_copy(src, dst, load_sem.at[i]))
        loads[-1].start()

    wanted = column(list_ref[...])
    rows = wanted.shape[0]
    pick = mask(wanted == lax.broadcasted_iota(jnp.int32, (rows, own), 1))
    packed[...] = dot(pick, nodes_ref[...])[: n_patch * slots].astype(BF16).reshape(packed.shape)
    patch[me_f] = nodes_ref[...]

    pl.semaphore_wait(barrier, len(bits) + n_patch - 1)

    def node_copy(have, bit):
        to = have | bit
        block = jnp.bitwise_xor(me_f, have)
        return pltpu.make_async_remote_copy(
            src_ref=nodes_ref if have == 0 else patch.at[block],
            dst_ref=patch.at[block],
            send_sem=node_send.at[to],
            recv_sem=node_recv.at[to],
            device_id=(me_p, feat_peer(bit)),
            device_id_type=MESH,
        )

    node_copies = {}
    for bit in reversed(bits):
        node_copies[bit] = node_copy(0, bit)
        node_copies[bit].start()
    list_copies = []
    for step in range(1, n_patch):
        to = patch_peer(step)
        copy = pltpu.make_async_remote_copy(
            src_ref=packed.at[to],
            dst_ref=remote.at[me_p],
            send_sem=list_send.at[step],
            recv_sem=list_recv.at[step],
            device_id=(to, me_f),
            device_id_type=MESH,
        )
        copy.start()
        list_copies.append(copy)
    remote[me_p] = packed[me_p]

    loads[0].wait()
    loads[1].wait()

    def first_part(at):
        span = pl.ds(pl.multiple_of(at * tile, tile), tile)
        first[span, :] = dot(edges_v[span, :], w1[:latent, :]) + b1_ref[...]

    halfway = (count // tile) // 2
    pl.loop(0, halfway)(first_part)

    for have in range(1, n_feat):
        if low_bit(have) > 1:
            node_copies[have].wait_recv()
            for bit in reversed([b for b in bits if b < low_bit(have)]):
                node_copies[have | bit] = node_copy(have, bit)
                node_copies[have | bit].start()

    pl.loop(halfway, count // tile)(first_part)

    for have in range(1, n_feat):
        if low_bit(have) == 1:
            node_copies[have].wait_recv()
    gathered = patch[...].reshape(n_local, latent)
    table[:n_local, :] = dot(gathered, w1[latent : 2 * latent, :]).astype(BF16)
    table[n_table:, :] = dot(gathered, w1[2 * latent :, :]).astype(BF16)
    for copy in list_copies:
        copy.wait_recv()
    listed = remote[...].reshape(n_patch * slots, latent)
    table[n_local:n_table, :] = dot(listed, w1[latent : 2 * latent, :]).astype(BF16)

    live = live_ref[0]
    loads[2].wait()

    def store(at):
        span = pl.ds(pl.multiple_of(at * tile, tile), tile)
        return pltpu.make_async_copy(out_v.at[span, :], edges_out.at[span, :], store_sem.at[at])

    def edge_part(at):
        span = pl.ds(pl.multiple_of(at * tile, tile), tile)
        receiver = column(recv_ref[:, span])
        slot = slot_ref[:, span]
        beyond = slot - n_local
        source = ((beyond.astype(F32) + 0.5) * (1.0 / cap)).astype(jnp.int32)
        slot = jnp.where(beyond < 0, slot, slot + source * (slots - cap))
        sender = column(slot)
        hits = jnp.concatenate(
            [
                mask(sender == lax.broadcasted_iota(jnp.int32, (tile, n_table), 1)),
                mask(receiver == lax.broadcasted_iota(jnp.int32, (tile, n_local), 1)),
            ],
            axis=1,
        )
        hidden = jax.nn.silu(first[span, :] + dot(hits, table[...])).astype(BF16)
        change = layer_norm(dot(hidden, w2[...]), gain_ref[...])
        place = lax.broadcasted_iota(jnp.int32, (tile, latent), 0) + at * tile
        change = jnp.where(place < live, change, 0.0)
        out_v[span, :] = (edges_v[span, :].astype(F32) + change).astype(BF16)
        store(at).start()

    pl.loop(0, count // tile)(edge_part)

    live_recv = jnp.where(
        lax.broadcasted_iota(jnp.int32, (1, count), 1) < live, recv_ref[...], -1
    )

    sum_copies = {}
    total = None
    for have in sorted(range(n_feat), key=lambda d: (low_bit(d) or n_feat, -d)):
        block = jnp.bitwise_xor(me_f, have)
        ids = lax.broadcasted_iota(jnp.int32, (own, count), 0) + block * own
        total = dot(mask(ids == live_recv), out_v[...])
        if have == 0:
            loads[3].wait()
            own_first = dot(nodes_ref[...], nw1[:latent, :]) + nb1_ref[...]
            loads[4].wait()
        for bit in bits:
            if have == 0 or bit < low_bit(have):
                sum_copies[have | bit].wait_recv()
                total = total + got_v[have | bit].astype(F32)
        if have:
            send_v[have] = total.astype(BF16)
            sum_copies[have] = pltpu.make_async_remote_copy(
                src_ref=send_v.at[have],
                dst_ref=got_v.at[have],
                send_sem=sum_send.at[have],
                recv_sem=sum_recv.at[have],
                device_id=(me_p, feat_peer(low_bit(have))),
                device_id_type=MESH,
            )
            sum_copies[have].start()

    hidden = jax.nn.silu(own_first + dot(total.astype(BF16), nw1[latent:, :])).astype(BF16)
    change = layer_norm(dot(hidden, nw2[...]), ngain_ref[...])
    nodes_out[...] = (nodes_ref[...].astype(F32) + change).astype(BF16)

    for copy in list(node_copies.values()) + list_copies + list(sum_copies.values()):
        copy.wait_send()
    for at in range(count // tile):
        store(at).wait()


def local(n_patch, n_feat, *args):
    (nodes, edges, receivers, sender_slot, send_rows, live_edges) = args[:6]
    (edge_w1, edge_b1, edge_w2, edge_gain, node_w1, node_b1, node_w2, node_gain) = args[6:]
    own, latent = nodes.shape
    count = edges.shape[0]
    cap = send_rows.shape[3]
    slots = -(-cap // 16) * 16
    while (n_feat * own + n_patch * slots) % LANES:
        slots += 16
    tile = next(t for t in (256, 128) if count % t == 0)
    listed = jnp.pad(send_rows[0, 0], ((0, 0), (0, slots - cap)), constant_values=-1)
    listed = listed.reshape(1, -1)
    listed = jnp.pad(listed, ((0, 0), (0, -listed.shape[1] % LANES)), constant_values=-1)
    n_table = n_feat * own + n_patch * slots
    vmem = pl.BlockSpec(memory_space=pltpu.VMEM)
    hbm = pl.BlockSpec(memory_space=pl.ANY)
    dma = pltpu.SemaphoreType.DMA
    return pl.pallas_call(
        functools.partial(kernel, n_patch, n_feat, cap, tile),
        out_shape=(
            jax.ShapeDtypeStruct(edges.shape, BF16),
            jax.ShapeDtypeStruct(nodes.shape, BF16),
        ),
        in_specs=[pl.BlockSpec(memory_space=pltpu.SMEM)] + [vmem] * 8 + [hbm] * 5,
        out_specs=(hbm, vmem),
        scratch_shapes=[
            pltpu.VMEM(edges.shape, BF16),
            pltpu.VMEM(edge_w1.shape, BF16),
            pltpu.VMEM(edge_w2.shape, BF16),
            pltpu.VMEM(node_w1.shape, BF16),
            pltpu.VMEM(node_w2.shape, BF16),
            pltpu.VMEM((n_patch, slots, latent), BF16),
            pltpu.VMEM((n_patch, slots, latent), BF16),
            pltpu.VMEM((n_feat, own, latent), BF16),
            pltpu.VMEM((n_table + n_feat * own, latent), BF16),
            pltpu.VMEM(edges.shape, F32),
            pltpu.VMEM(edges.shape, BF16),
            pltpu.VMEM((n_feat, own, latent), BF16),
            pltpu.VMEM((n_feat, own, latent), BF16),
            dma((5,)),
            dma((count // tile,)),
            dma((n_patch,)),
            dma((n_patch,)),
            dma((n_feat,)),
            dma((n_feat,)),
            dma((n_feat,)),
            dma((n_feat,)),
        ],
        compiler_params=pltpu.CompilerParams(
            collective_id=0, has_side_effects=True, vmem_limit_bytes=60 * 1024 * 1024
        ),
    )(
        live_edges,
        nodes,
        receivers.reshape(1, -1),
        sender_slot.reshape(1, -1),
        listed,
        edge_b1.reshape(1, -1),
        edge_gain.reshape(1, -1),
        node_b1.reshape(1, -1),
        node_gain.reshape(1, -1),
        edges,
        edge_w1,
        edge_w2,
        node_w1,
        node_w2,
    )


def solution(mesh):
    both = P(("patch", "feat"))
    rows = P(("patch", "feat"), None)
    placed = (rows, rows, both, both, P("patch", "feat", None, None), both) + (P(),) * 8
    return jax.shard_map(
        functools.partial(local, mesh.shape["patch"], mesh.shape["feat"]),
        mesh=mesh,
        in_specs=placed,
        out_specs=(rows, rows),
        check_vma=False,
    )
```

time: 93.8 us -> 38.1 us (0.41)
  Pallas kernels: 0 us -> 29.4 us
  waiting for transfers between devices: 24.3 us -> 0 us
  matrix products: 16 us -> 0 us
  between operations: 14.9 us -> 1.3 us
  local copies, waits for them, and re-layouts: 18.5 us -> 7.09 us
  blocking collectives: 7.91 us -> 0 us
  starting transfers between devices: 7.32 us -> 0 us
  other arithmetic: 4.5 us -> 0 us
    pallas_call x0 -> x1, Pallas kernels: none -> 29.4 us  [local(): pl.pallas_call(functools.partial(kernel, n_patch, n_feat, cap, tile), out...]
    reduce_scatter x1 -> x0, waiting for transfers between devices: 24.3 us -> none  [local(): lax.psum_scatter(partial_sums, 'feat', scatter_dimension=0, tiled=True)]
    dot_general x6 -> x0, matrix products: 16 us -> none  [the longest x1 4.35 us: edge_change(): jnp.dot(sender_feat, edge_w1[latent:2 * latent], preferred_element_type=j...]
    gather x3 -> x0, local copies, waits for them, and re-layouts: 10.9 us -> none  [the longest x1 4.72 us: local(): receiver_feat = jnp.take(patch_rows, receivers, axis=0)]
    all_gather x1 -> x0, blocking collectives: 7.91 us -> none  [local(): patch_rows = lax.all_gather(nodes, 'feat', axis=0, tiled=True)]
    all_to_all x1 -> x0, starting transfers between devices: 7.28 us -> none  [local(): lax.all_to_all(packed, 'patch', split_axis=0, concat_axis=0, tiled=True)]
    unnamed x30 -> x4, local copies, waits for them, and re-layouts: 6.7 us -> 3.16 us
    reshape x0 -> x3, local copies, waits for them, and re-layouts: none -> 3.24 us  [the longest x1 1.29 us: local(): receivers.reshape(1, -1)]
  transfers between devices with their start and end apart: 2 -> 0, of which waited for: 1 -> 0; matrix products, arithmetic and copies ran while one was open for 12% -> 0% of each run, Pallas kernels for 0% -> 0%
where the time goes in v1:
time: 38.1 us; the launch traced here: 37.8 us
  Pallas kernels  29.4 us (77%)
  local copies, waits for them, and re-layouts  7.09 us (19%)
  between operations  1.3 us (3%)
    pallas_call x1, Pallas kernels, local(): pl.pallas_call(functools.partial(kernel, n_patch, n_feat, cap, tile), out...  29.4 us
    unnamed x4, local copies, waits for them, and re-layouts  3.16 us
    reshape x1, local copies, waits for them, and re-layouts, local(): receivers.reshape(1, -1)  1.29 us
    reshape x1, local copies, waits for them, and re-layouts, local(): sender_slot.reshape(1, -1)  1.29 us

profile of v1, /device:TPU:0, one launch (start us, length us, event | category | flops | bytes accessed | tf_op | source)
XLA Modules:
  0.0 37.8 jit_solution(10030148536343719721)
XLA Ops:
  1.3 0.7 %pad.4 = s32[8,32]{1,0:T(8,128)S(1)} pad(s32[8,24]{1,0:T(8,128)} %bitcast.5, s32[]{:T(128)} %constant.0.clone.1), padding=0_0x0_8 | pad | bytes 1796 | tf_op jit(solution)/shard_map/jit(_pad)/pad | solution.py:267
  2.0 0.7 %reshape.27.list_ref = s32[1,256]{1,0:T(1,128)} reshape(s32[8,32]{1,0:T(8,128)S(1)} %pad.4) | data formatting | bytes 2048 | tf_op jit(solution)/shard_map/reshape | solution.py:268
  2.6 1.3 %reshape.25.recv_ref = s32[1,1280]{1,0:T(1,128)} reshape(s32[1280]{0:T(1024)} %param.16) | data formatting | bytes 10240 | tf_op jit(solution)/shard_map/reshape | solution.py:311
  3.9 1.3 %reshape.26.slot_ref = s32[1,1280]{1,0:T(1,128)} reshape(s32[1280]{0:T(1024)} %param.17) | data formatting | bytes 10240 | tf_op jit(solution)/shard_map/reshape | solution.py:312
  5.2 29.4 %shard_map.149 = (bf16[1280,512]{1,0:T(8,128)(2,1)}, bf16[160,512]{1,0:T(8,128)(2,1)}) custom-call(s32[1]{0:T(128)S(6)} %copy.18.live_ref, bf16[160,512]{1,0:T(8,128)(2,1)} %nodes_ref.1, s32[1,1280]{1,0:T(1,128)} %reshape.25.recv_ref, s32[1,1280]{1,0:T(1,128)} %reshape.26.slot_ref, s32[1,256]{1,0:T(1,128)} %reshape.27.list_ref, f32[1,512]{1,0:T(1,128)} %bitcast.6, ...), custom_call_target="tpu_custom_call" | custom-call | tf_op jit(solution)/shard_map/pallas_call | solution.py:274
  34.6 0.0 copy-start
  34.6 2.5 %copy.19 = bf16[1280,512]{1,0:T(8,128)(2,1)} copy(bf16[1280,512]{1,0:T(8,128)(2,1)} %get-tuple-element.4) | data formatting | bytes 2621440
  37.1 0.0 copy-done
  37.1 0.7 %copy.20 = bf16[160,512]{1,0:T(8,128)(2,1)} copy(bf16[160,512]{1,0:T(8,128)(2,1)S(1)} %copy-done) | data formatting | bytes 327680
Async XLA Ops:
  34.6 2.5 %copy-start = (bf16[160,512]{1,0:T(8,128)(2,1)S(1)}, bf16[160,512]{1,0:T(8,128)(2,1)}, u32[]{:S(2)}) copy-start(bf16[160,512]{1,0:T(8,128)(2,1)} %get-tuple-element.5) | copy-start | bytes 491524

commit v2 on v1

--- a/solution.py
+++ b/solution.py
@@ -24,11 +24,8 @@
     return centred * lax.rsqrt(variance + epsilon) * scales
 
 
-def column(row):
-    parts = []
-    for at in range(0, row.shape[1], LANES):
-        block = jnp.broadcast_to(row[:, at : at + LANES], (LANES, LANES))
-        parts.append(block.T[:, :1])
+def column(rows):
+    parts = [jnp.broadcast_to(row, (LANES, LANES)).T[:, :1] for row in rows]
     return jnp.concatenate(parts, axis=0)
 
 
@@ -71,6 +68,8 @@
     patch,
     table,
     first,
+    hits,
+    grid_v,
     out_v,
     send_v,
     got_v,
@@ -114,12 +113,6 @@
         loads.append(pltpu.make_async_copy(src, dst, load_sem.at[i]))
         loads[-1].start()
 
-    wanted = column(list_ref[...])
-    rows = wanted.shape[0]
-    pick = mask(wanted == lax.broadcasted_iota(jnp.int32, (rows, own), 1))
-    packed[...] = dot(pick, nodes_ref[...])[: n_patch * slots].astype(BF16).reshape(packed.shape)
-    patch[me_f] = nodes_ref[...]
-
     pl.semaphore_wait(barrier, len(bits) + n_patch - 1)
 
     def node_copy(have, bit):
@@ -138,6 +131,37 @@
     for bit in reversed(bits):
         node_copies[bit] = node_copy(0, bit)
         node_copies[bit].start()
+    grid_v[...] = jnp.full(grid_v.shape, -1, jnp.int32)
+    grid_v[:n_patch, :cap] = list_ref[...]
+    lists = grid_v[...].T
+    wanted = jnp.concatenate([lists[:slots, p : p + 1] for p in range(n_patch)], axis=0)
+    pick = mask(wanted == lax.broadcasted_iota(jnp.int32, (n_patch * slots, own), 1))
+    packed[...] = dot(pick, nodes_ref[...]).astype(BF16).reshape(packed.shape)
+    patch[me_f] = nodes_ref[...]
+
+    per_tile = tile // LANES
+
+    def hit_part(at):
+        span = pl.ds(pl.multiple_of(at * tile, tile), tile)
+        lines = [pl.ds(at * per_tile + i, 1) for i in range(per_tile)]
+        receiver = column([recv_ref[line, :] for line in lines])
+        senders = []
+        for line in lines:
+            slot = slot_ref[line, :]
+            beyond = slot - n_local
+            source = ((beyond.astype(F32) + 0.5) * (1.0 / cap)).astype(jnp.int32)
+            senders.append(jnp.where(beyond < 0, slot, slot + source * (slots - cap)))
+        sender = column(senders)
+        hits[span, :n_table] = mask(
+            sender == lax.broadcasted_iota(jnp.int32, (tile, n_table), 1)
+        )
+        hits[span, n_table:] = mask(
+            receiver == lax.broadcasted_iota(jnp.int32, (tile, n_local), 1)
+        )
+
+    halfway = (count // tile) // 2
+    pl.loop(0, halfway)(hit_part)
+
     list_copies = []
     for step in range(1, n_patch):
         to = patch_peer(step)
@@ -160,8 +184,7 @@
         span = pl.ds(pl.multiple_of(at * tile, tile), tile)
         first[span, :] = dot(edges_v[span, :], w1[:latent, :]) + b1_ref[...]
 
-    halfway = (count // tile) // 2
-    pl.loop(0, halfway)(first_part)
+    pl.loop(0, count // tile)(first_part)
 
     for have in range(1, n_feat):
         if low_bit(have) > 1:
@@ -170,7 +193,7 @@
                 node_copies[have | bit] = node_copy(have, bit)
                 node_copies[have | bit].start()
 
-    pl.loop(halfway, count // tile)(first_part)
+    pl.loop(halfway, count // tile)(hit_part)
 
     for have in range(1, n_feat):
         if low_bit(have) == 1:
@@ -192,20 +215,7 @@
 
     def edge_part(at):
         span = pl.ds(pl.multiple_of(at * tile, tile), tile)
-        receiver = column(recv_ref[:, span])
-        slot = slot_ref[:, span]
-        beyond = slot - n_local
-        source = ((beyond.astype(F32) + 0.5) * (1.0 / cap)).astype(jnp.int32)
-        slot = jnp.where(beyond < 0, slot, slot + source * (slots - cap))
-        sender = column(slot)
-        hits = jnp.concatenate(
-            [
-                mask(sender == lax.broadcasted_iota(jnp.int32, (tile, n_table), 1)),
-                mask(receiver == lax.broadcasted_iota(jnp.int32, (tile, n_local), 1)),
-            ],
-            axis=1,
-        )
-        hidden = jax.nn.silu(first[span, :] + dot(hits, table[...])).astype(BF16)
+        hidden = jax.nn.silu(first[span, :] + dot(hits[span, :], table[...])).astype(BF16)
         change = layer_norm(dot(hidden, w2[...]), gain_ref[...])
         place = lax.broadcasted_iota(jnp.int32, (tile, latent), 0) + at * tile
         change = jnp.where(place < live, change, 0.0)
@@ -214,16 +224,18 @@
 
     pl.loop(0, count // tile)(edge_part)
 
-    live_recv = jnp.where(
-        lax.broadcasted_iota(jnp.int32, (1, count), 1) < live, recv_ref[...], -1
-    )
+    live_recv = []
+    for line in range(count // LANES):
+        place = lax.broadcasted_iota(jnp.int32, (1, LANES), 1) + line * LANES
+        live_recv.append(jnp.where(place < live, recv_ref[line : line + 1, :], -1))
 
     sum_copies = {}
     total = None
     for have in sorted(range(n_feat), key=lambda d: (low_bit(d) or n_feat, -d)):
         block = jnp.bitwise_xor(me_f, have)
-        ids = lax.broadcasted_iota(jnp.int32, (own, count), 0) + block * own
-        total = dot(mask(ids == live_recv), out_v[...])
+        ids = lax.broadcasted_iota(jnp.int32, (own, LANES), 0) + block * own
+        spread = jnp.concatenate([mask(ids == line) for line in live_recv], axis=1)
+        total = dot(spread, out_v[...])
         if have == 0:
             loads[3].wait()
             own_first = dot(nodes_ref[...], nw1[:latent, :]) + nb1_ref[...]
@@ -264,9 +276,6 @@
     while (n_feat * own + n_patch * slots) % LANES:
         slots += 16
     tile = next(t for t in (256, 128) if count % t == 0)
-    listed = jnp.pad(send_rows[0, 0], ((0, 0), (0, slots - cap)), constant_values=-1)
-    listed = listed.reshape(1, -1)
-    listed = jnp.pad(listed, ((0, 0), (0, -listed.shape[1] % LANES)), constant_values=-1)
     n_table = n_feat * own + n_patch * slots
     vmem = pl.BlockSpec(memory_space=pltpu.VMEM)
     hbm = pl.BlockSpec(memory_space=pl.ANY)
@@ -290,6 +299,8 @@
             pltpu.VMEM((n_feat, own, latent), BF16),
             pltpu.VMEM((n_table + n_feat * own, latent), BF16),
             pltpu.VMEM(edges.shape, F32),
+            pltpu.VMEM((count, n_table + n_feat * own), BF16),
+            pltpu.VMEM((LANES, LANES), jnp.int32),
             pltpu.VMEM(edges.shape, BF16),
             pltpu.VMEM((n_feat, own, latent), BF16),
             pltpu.VMEM((n_feat, own, latent), BF16),
@@ -308,9 +319,9 @@
     )(
         live_edges,
         nodes,
-        receivers.reshape(1, -1),
-        sender_slot.reshape(1, -1),
-        listed,
+        receivers.reshape(-1, LANES),
+        sender_slot.reshape(-1, LANES),
+        send_rows[0, 0],
         edge_b1.reshape(1, -1),
         edge_gain.reshape(1, -1),
         node_b1.reshape(1, -1),

time: 38.1 us -> 32.9 us (0.86)
  local copies, waits for them, and re-layouts: 7.09 us -> 3.16 us
  Pallas kernels: 29.4 us -> 28.2 us
    reshape x3 -> x0, local copies, waits for them, and re-layouts: 3.24 us -> none  [the longest x1 1.29 us: local(): receivers.reshape(1, -1)]
    pallas_call x1, Pallas kernels: 29.4 us -> 28.2 us  [local(): pl.pallas_call(functools.partial(kernel, n_patch, n_feat, cap, tile), out...]
    pad x1 -> x0, local copies, waits for them, and re-layouts: 0.69 us -> none  [local(): jnp.pad(send_rows[0, 0], ((0, 0), (0, slots - cap)), constant_values=-1)]
where the time goes in v2:
time: 32.9 us; the launch traced here: 32.7 us
  Pallas kernels  28.2 us (86%)
  local copies, waits for them, and re-layouts  3.16 us (10%)
  between operations  1.3 us (4%)
    pallas_call x1, Pallas kernels, local(): pl.pallas_call(functools.partial(kernel, n_patch, n_feat, cap, tile), out...  28.2 us
    unnamed x4, local copies, waits for them, and re-layouts  3.16 us

profile of v2, /device:TPU:0, one launch (start us, length us, event | category | flops | bytes accessed | tf_op | source)
XLA Modules:
  0.0 32.7 jit_solution(4663817055832682833)
XLA Ops:
  1.3 28.2 %shard_map.149 = (bf16[1280,512]{1,0:T(8,128)(2,1)}, bf16[160,512]{1,0:T(8,128)(2,1)}) custom-call(s32[1]{0:T(128)S(6)} %copy.18.live_ref, bf16[160,512]{1,0:T(8,128)(2,1)} %nodes_ref.1, s32[10,128]{1,0:T(8,128)} %bitcast.7, s32[10,128]{1,0:T(8,128)} %bitcast.8, s32[8,24]{1,0:T(8,128)} %bitcast.9, f32[1,512]{1,0:T(1,128)} %bitcast.10, f32[1,512]{1,0:T(1,128)} %bitcast.11, ...), custom_call_target="tpu_custom_call" | custom-call | tf_op jit(solution)/shard_map/pallas_call | solution.py:283
  29.5 0.0 copy-start
  29.5 2.5 %copy.19 = bf16[1280,512]{1,0:T(8,128)(2,1)} copy(bf16[1280,512]{1,0:T(8,128)(2,1)} %get-tuple-element.4) | data formatting | bytes 2621440
  32.0 0.0 copy-done
  32.0 0.7 %copy.20 = bf16[160,512]{1,0:T(8,128)(2,1)} copy(bf16[160,512]{1,0:T(8,128)(2,1)S(1)} %copy-done) | data formatting | bytes 327680
Async XLA Ops:
  29.5 2.5 %copy-start = (bf16[160,512]{1,0:T(8,128)(2,1)S(1)}, bf16[160,512]{1,0:T(8,128)(2,1)}, u32[]{:S(2)}) copy-start(bf16[160,512]{1,0:T(8,128)(2,1)} %get-tuple-element.5) | copy-start | bytes 491524
